TPU v7x, 32 devices: a whole 2x2x4 slice. The times are simulated.
32 devices in a mesh: req: 8 (over z, y), tp: 4 (over x, core).
Axes of the slice: x: 2, y: 2, z: 4, core: 2. Of those that a mesh axis runs over, the one named last changes fastest.
Arguments:
- tokens: bfloat16 [16384, 8192], P('req', 'tp'), may hold values from -6 to 6
- base_projection_weight: bfloat16 [8192, 2048], P('tp'), may hold values from -0.0625 to 0.0625
- adapter_down_maps: bfloat16 [128, 8192, 128], P('req', 'tp'), may hold values from -0.0625 to 0.0625
- adapter_up_maps: bfloat16 [128, 64, 2048], P('req', None, 'tp'), may hold values from -0.75 to 0.75
- block_adapter_ids: int32 [128], replicated, may hold values from 0 to 128, as said below
- adapter_storage_entry: int32 [128], replicated, may hold values from 0 to 127, as said below
Outputs:
- key_value: bfloat16 [16384, 2048], P('req', 'tp')
Inputs may be any that keep to these rules, and one draw needn't show every extreme that they name: `block_adapter_ids`: ids are 0 (base model) or 1 to 128. Adapter k is held by req index adapter_storage_entry[k - 1] // 16. Among the 16 blocks of one req index (blocks i * 16 to i * 16 + 15) at most 2 name adapters held by any one req index; in every draw one req index receives exactly 2 blocks, all naming one adapter, from every req index. `adapter_storage_entry`: A permutation: each storage entry holds exactly one adapter.
All inputs are finite; a program needn't handle non-finite values.
Results may differ from a plain program's by a relative error of at most 0.014.
Values may be sent and summed in bfloat16 or wider, within the bound.
A program may use at most 128 MiB of HBM per device.

v0:
```python
import jax
import jax.numpy as jnp
from jax import lax
from jax.sharding import PartitionSpec as P

KEY_WIDTH = 1024
BLOCK = 128
CAP = 2


def per_device(
    tokens,
    base_projection_weight,
    adapter_down_maps,
    adapter_up_maps,
    block_adapter_ids,
    adapter_storage_entry,
):
    req_count = lax.axis_size("req")
    my_req = lax.axis_index("req")
    my_tp = lax.axis_index("tp")
    row_count, feat_count = tokens.shape
    blk_count = row_count // BLOCK
    adapter_count = adapter_down_maps.shape[0]
    rank_width = adapter_up_maps.shape[1]
    column_count = adapter_up_maps.shape[2]
    half_index = my_tp * column_count // KEY_WIDTH
    tok_blocks = tokens.reshape(blk_count, BLOCK, feat_count)
    partial_value = jnp.dot(tokens, base_projection_weight, preferred_element_type=jnp.float32)
    base_sum = lax.psum_scatter(
        partial_value.astype(jnp.bfloat16), "tp", scatter_dimension=1, tiled=True
    ).astype(jnp.float32)
    ids_all = block_adapter_ids.reshape(req_count, blk_count)
    stored = adapter_storage_entry[jnp.maximum(ids_all - 1, 0)]
    owner_all = jnp.where(ids_all > 0, stored // adapter_count, -1)
    local_all = stored % adapter_count
    block_pos = jnp.arange(blk_count, dtype=jnp.int32)
    before = block_pos[None, :] < block_pos[:, None]
    same_owner = owner_all[:, :, None] == owner_all[:, None, :]
    slot_all = jnp.sum(same_owner & before[None], axis=2)
    ids_own = lax.dynamic_index_in_dim(ids_all, my_req, 0, keepdims=False)
    owner_own = lax.dynamic_index_in_dim(owner_all, my_req, 0, keepdims=False)
    slot_own = lax.dynamic_index_in_dim(slot_all, my_req, 0, keepdims=False)
    spot_index = jnp.maximum(owner_own, 0) * CAP + slot_own
    owner_ids = jnp.arange(req_count, dtype=jnp.int32)[:, None, None]
    slot_ids = jnp.arange(CAP, dtype=jnp.int32)[None, :, None]
    incoming = (owner_all[:, None, :] == my_req) & (slot_all[:, None, :] == slot_ids)
    in_valid = jnp.any(incoming, axis=2)
    input_resident = jnp.sum(jnp.where(incoming, local_all[:, None, :], 0), axis=2)
    outgoing = (owner_own[None, None, :] == owner_ids) & (slot_own[None, None, :] == slot_ids)
    out_valid = jnp.any(outgoing, axis=2)
    pick_block = jnp.sum(jnp.where(outgoing, block_pos[None, None, :], 0), axis=2)
    send_rows = jnp.where(
        out_valid[:, :, None, None], tok_blocks[pick_block], jnp.zeros((), tokens.dtype)
    )
    landed_rows = lax.all_to_all(send_rows, "req", split_axis=0, concat_axis=0, tiled=True)
    partial_shrink = jnp.einsum(
        "vhyf,vhfp->vhyp",
        landed_rows,
        adapter_down_maps[input_resident],
        preferred_element_type=jnp.float32,
    )
    down_projected = lax.psum(partial_shrink.astype(jnp.bfloat16), "tp")
    down_projected_half = lax.dynamic_slice_in_dim(
        down_projected, half_index * rank_width, rank_width, 3
    )
    adapter_delta = jnp.einsum(
        "zflj,zfjb->zflb",
        down_projected_half,
        adapter_up_maps[input_resident],
        preferred_element_type=jnp.float32,
    ).astype(jnp.bfloat16)
    adapter_delta = jnp.where(
        in_valid[:, :, None, None], adapter_delta, jnp.zeros((), jnp.bfloat16)
    )
    returned = lax.all_to_all(adapter_delta, "req", split_axis=0, concat_axis=0, tiled=True)
    own_delta = returned.reshape(req_count * CAP, BLOCK, column_count)[spot_index]
    own_delta = jnp.where(ids_own[:, None, None] > 0, own_delta, jnp.zeros((), jnp.bfloat16))
    return (base_sum + own_delta.reshape(row_count, column_count).astype(jnp.float32)).astype(
        jnp.bfloat16
    )


def solution(mesh):
    placed = (P("req", "tp"), P("tp", None), P("req", "tp", None), P("req", None, "tp"), P(), P())
    return jax.shard_map(
        per_device, mesh=mesh, in_specs=placed, out_specs=P("req", "tp"), check_vma=False
    )
```

profile of v0, /device:TPU:0, one launch (start us, length us, event | category | flops | bytes accessed | tf_op | source)
XLA Modules:
  0.0 343.1 jit_solution(5026651904690158362)
XLA Ops:
  6.5 0.7 add_maximum_fusion
  7.3 0.7 reshape.232
  8.0 1.6 gather_fusion
  9.7 0.3 convert_reduce_fusion
  10.1 0.1 fusion.1
  10.2 0.2 and_reduce_fusion
  10.4 0.2 select_reduce_fusion
  10.8 8.1 %gather_fusion.1 = bf16[16,128,2048]{2,1,0:T(8,128)(2,1)} fusion(bf16[16,128,2048]{2,1,0:T(8,128)(2,1)} %bitcast.36, s32[1024]{0:T(1024)S(1)} %pad_clamp_fusion.2), kind=kCustom, calls=%fused_computation.1 | custom fusion | bytes 16777280 | tf_op jit(solution)/shard_map/gather | solution.py:54
  19.0 7.2 %broadcast_select_fusion = bf16[8,2,128,2048]{3,2,1,0:T(8,128)(2,1)} fusion(bf16[8,2,128,2048]{3,2,1,0:T(8,128)(2,1)} %bitcast.35, pred[8,2]{1,0:T(8,128)(4,1)S(1)} %copy.12), kind=kLoop, calls=%fused_computation.5 | loop fusion | flops 4194304 | bytes 16777232 | tf_op jit(solution)/shard_map/jit(_where)/select_n | solution.py:53
  26.2 7.3 %all-to-all-start = ((bf16[8,2,128,2048]{3,2,1,0:T(8,128)(2,1)}), bf16[8,2,128,2048]{3,2,1,0:T(8,128)(2,1)}, u32[]{:S(2)}, u32[]{:S(2)}) async-start(bf16[8,2,128,2048]{3,2,1,0:T(8,128)(2,1)} %broadcast_select_fusion), calls=%async_computation.1 | async-start | bytes 16777216 | tf_op jit(solution)/shard_map/all_to_all | solution.py:56
  33.7 8.1 %gather_fusion.2 = bf16[16,2048,128]{2,1,0:T(8,128)(2,1)} fusion(bf16[16,2048,128]{2,1,0:T(8,128)(2,1)} %param.8, s32[1024]{0:T(1024)S(1)} %pad_clamp_fusion.1), kind=kCustom, calls=%fused_computation.2 | custom fusion | bytes 16777280 | tf_op jit(solution)/shard_map/gather | solution.py:60
  41.8 174.8 %all-to-all-done = bf16[8,2,128,2048]{3,2,1,0:T(8,128)(2,1)} async-done(((bf16[8,2,128,2048]{3,2,1,0:T(8,128)(2,1)}), bf16[8,2,128,2048]{3,2,1,0:T(8,128)(2,1)}, u32[]{:S(2)}, u32[]{:S(2)}) %all-to-all-start) | async-done | bytes 8388640 | tf_op jit(solution)/shard_map/all_to_all | solution.py:56
  216.6 9.4 %convolution_convert_fusion.1 = bf16[8,2,128,128]{2,3,1,0:T(8,128)(2,1)} fusion(bf16[8,2,128,2048]{3,2,1,0:T(8,128)(2,1)} %all-to-all-done, bf16[8,2,2048,128]{3,2,1,0:T(8,128)(2,1)} %bitcast.34), kind=kOutput, calls=%fused_computation.10 | convolution fusion | flops 1074003968 | bytes 17301504 | tf_op jit(solution)/shard_map/vhyf,vhfp->vhyp/dot_general | solution.py:57
  226.1 23.6 %convolution_convert_fusion = bf16[2048,2048]{1,0:T(8,128)(2,1)} fusion(bf16[2048,2048]{1,0:T(8,128)(2,1)} %param.6, bf16[2048,2048]{1,0:T(8,128)(2,1)} %param.7), kind=kOutput, calls=%fused_computation.6 | convolution fusion | flops 17184063488 | bytes 25165824 | tf_op jit(solution)/shard_map/dot_general | solution.py:29
  249.7 0.6 gather_fusion.3
  250.3 0.1 fusion.3
  250.5 0.1 copy.11
  250.6 7.8 %all-reduce.2.cloned.1.call-done = bf16[8,2,128,128]{2,3,1,0:T(8,128)(2,1)} async-done(((bf16[8,2,128,128]{2,3,1,0:T(8,128)(2,1)}), bf16[8,2,128,128]{2,3,1,0:T(8,128)(2,1)}) %all-reduce.2.cloned.1.call-update) | async-done | bytes 524304 | tf_op jit(solution)/shard_map/psum | solution.py:63
  258.4 3.1 convert_select_fusion
  261.5 5.5 %all-to-all-start.1 = ((bf16[8,2,128,512]{3,2,1,0:T(8,128)(2,1)}), bf16[8,2,128,512]{3,2,1,0:T(8,128)(2,1)S(1)}, u32[]{:S(2)}, u32[]{:S(2)}) async-start(bf16[8,2,128,512]{3,2,1,0:T(8,128)(2,1)} %convert_select_fusion), calls=%async_computation.2 | async-start | bytes 4194304 | tf_op jit(solution)/shard_map/all_to_all | solution.py:76
  267.1 47.2 %all-to-all-done.1 = bf16[8,2,128,512]{3,2,1,0:T(8,128)(2,1)S(1)} async-done(((bf16[8,2,128,512]{3,2,1,0:T(8,128)(2,1)}), bf16[8,2,128,512]{3,2,1,0:T(8,128)(2,1)S(1)}, u32[]{:S(2)}, u32[]{:S(2)}) %all-to-all-start.1) | async-done | bytes 2097184 | tf_op jit(solution)/shard_map/all_to_all | solution.py:76
  314.3 2.0 gather_fusion.4
  316.3 16.4 %reduce-scatter.2.cloned.1.call-done = bf16[2048,512]{1,0:T(8,128)(2,1)} async-done(((bf16[2048,2048]{1,0:T(8,128)(2,1)}), bf16[2048,512]{1,0:T(8,128)(2,1)}) %reduce-scatter.2.cloned.1.call-update) | async-done | bytes 2097168 | tf_op jit(solution)/shard_map/reduce_scatter | solution.py:30
  332.7 3.5 %add_convert_fusion = bf16[2048,512]{1,0:T(8,128)(2,1)} fusion(bf16[2048,512]{1,0:T(8,128)(2,1)} %reduce-scatter.2.cloned.1.call-done, bf16[16,128,512]{2,1,0:T(8,128)(2,1)} %gather_fusion.4, pred[2048]{0:T(1024)(128)(4,1)S(1)} %broadcast_bitcast_fusion), kind=kLoop, calls=%fused_computation.7 | loop fusion | flops 5242880 | bytes 6293504 | tf_op jit(solution)/shard_map/convert_element_type | solution.py:79
  (27 shorter events, 0.8 us)
Async XLA Ops:
  6.5 243.2 %copy-start = (bf16[16,64,512]{2,1,0:T(8,128)(2,1)S(1)}, bf16[16,64,512]{2,1,0:T(8,128)(2,1)}, u32[]{:S(2)}) copy-start(bf16[16,64,512]{2,1,0:T(8,128)(2,1)} %param.9) | copy-start | bytes 3145732
  26.2 190.4 %all-to-all-start = ((bf16[8,2,128,2048]{3,2,1,0:T(8,128)(2,1)}), bf16[8,2,128,2048]{3,2,1,0:T(8,128)(2,1)}, u32[]{:S(2)}, u32[]{:S(2)}) async-start(bf16[8,2,128,2048]{3,2,1,0:T(8,128)(2,1)} %broadcast_select_fusion), calls=%async_computation.1 | async-start | bytes 16777216 | tf_op jit(solution)/shard_map/all_to_all | solution.py:56
  33.5 224.9 %all-reduce.2.cloned.1.call-start = ((), (), s32[]{:S(2)}) async-start(), calls=%async_computation.4 | async-start | bytes 1048576 | tf_op jit(solution)/shard_map/psum | solution.py:63
  226.0 106.7 %reduce-scatter.2.cloned.1.call-start = ((), (), s32[]{:S(2)}) async-start(), calls=%async_computation.3 | async-start | bytes 10485760 | tf_op jit(solution)/shard_map/reduce_scatter | solution.py:30
  261.5 52.8 %all-to-all-start.1 = ((bf16[8,2,128,512]{3,2,1,0:T(8,128)(2,1)}), bf16[8,2,128,512]{3,2,1,0:T(8,128)(2,1)S(1)}, u32[]{:S(2)}, u32[]{:S(2)}) async-start(bf16[8,2,128,512]{3,2,1,0:T(8,128)(2,1)} %convert_select_fusion), calls=%async_computation.2 | async-start | bytes 4194304 | tf_op jit(solution)/shard_map/all_to_all | solution.py:76
Sparse Core Ops, SparseCore 0:
  226.1 32.2 all-reduce.1
  261.0 71.7 reduce-scatter.1
where the time goes:
time: 344 us; the launch traced here: 343 us
  waiting for transfers between devices  246 us (72%)
  matrix products  36 us (10%)
  local copies, waits for them, and re-layouts  21.9 us (6%)
  between operations  13.5 us (4%)
  starting transfers between devices  12.9 us (4%)
  other arithmetic  12.5 us (4%)
    all_to_all x1, waiting for transfers between devices, per_device(): lax.all_to_all(send_rows, 'req', split_axis=0, concat_axis=0, tiled=True)  175 us
    all_to_all x1, waiting for transfers between devices, per_device(): lax.all_to_all(adapter_delta, 'req', split_axis=0, concat_axis=0, tiled=T...  47.2 us
    dot_general x1, matrix products, per_device(): jnp.dot(tokens, base_projection_weight, preferred_element_type=jnp.float32)  23.6 us
    reduce_scatter x1, waiting for transfers between devices, per_device(): lax.psum_scatter(partial_value.astype(jnp.bfloat16), 'tp', scatter_dimens...  16.4 us
    dot_general x1, matrix products, per_device(): jnp.einsum('vhyf,vhfp->vhyp', landed_rows, adapter_down_maps[input_reside...  9.37 us
    gather x1, local copies, waits for them, and re-layouts, per_device(): adapter_down_maps[input_resident]  8.15 us
    gather x1, local copies, waits for them, and re-layouts, per_device(): tok_blocks[pick_block]  8.14 us
    psum x1, waiting for transfers between devices, per_device(): down_projected = lax.psum(partial_shrink.astype(jnp.bfloat16), 'tp')  7.84 us
  transfers between devices with their start and end apart: 4, of which 4 were waited for; matrix products, arithmetic and copies ran while one was open for 11% of the time, Pallas kernels for 0%

commit v1 on v0

v1 whole, which is shorter than its diff:
```python
import functools

import jax
import jax.numpy as jnp
from jax import lax
from jax.experimental import pallas as pl
from jax.experimental.pallas import tpu as pltpu
from jax.sharding import PartitionSpec as P

KEY_WIDTH = 1024
BLOCK = 128
CAP = 2


def shrink_body(blk_ref, tok_a, tok_b, down_a, down_b, out_ref):
    rank = out_ref.shape[-1] // 2
    one = jnp.dot(tok_a[...], down_a[0], preferred_element_type=jnp.float32).astype(out_ref.dtype)
    two = jnp.dot(tok_b[...], down_b[0], preferred_element_type=jnp.float32).astype(out_ref.dtype)
    out_ref[0, 0] = jnp.concatenate([one[:, :rank], two[:, :rank]], axis=1)
    out_ref[1, 0] = jnp.concatenate([one[:, rank:], two[:, rank:]], axis=1)


def shrink_pairs(tokens, downs, blk_of):
    items, feat, width = downs.shape
    pairs = items // 2
    return pl.pallas_call(
        shrink_body,
        grid_spec=pltpu.PrefetchScalarGridSpec(
            num_scalar_prefetch=1,
            grid=(pairs,),
            in_specs=[
                pl.BlockSpec((BLOCK, feat), lambda p, blk: (blk[2 * p], 0)),
                pl.BlockSpec((BLOCK, feat), lambda p, blk: (blk[2 * p + 1], 0)),
                pl.BlockSpec((1, feat, width), lambda p, blk: (2 * p, 0, 0)),
                pl.BlockSpec((1, feat, width), lambda p, blk: (2 * p + 1, 0, 0)),
            ],
            out_specs=pl.BlockSpec((2, 1, BLOCK, width), lambda p, blk: (0, p, 0, 0)),
        ),
        out_shape=jax.ShapeDtypeStruct((2, pairs, BLOCK, width), tokens.dtype),
        cost_estimate=pl.CostEstimate(
            flops=2 * items * BLOCK * feat * width,
            bytes_accessed=2 * items * feat * (BLOCK + width),
            transcendentals=0,
        ),
    )(blk_of, tokens, tokens, downs, downs)


def finish_body(spot_ref, live_ref, base_ref, shrink_ref, up_ref, out_ref):
    b = pl.program_id(0)
    rank = up_ref.shape[1]
    odd = spot_ref[b] % 2
    both = shrink_ref[0]
    mine = jnp.where(odd == 1, both[:, rank:], both[:, :rank])
    delta = jnp.dot(mine, up_ref[0], preferred_element_type=jnp.float32)
    delta = delta.astype(jnp.bfloat16).astype(jnp.float32)
    delta = jnp.where(live_ref[b] > 0, delta, jnp.zeros_like(delta))
    out_ref[...] = (base_ref[...].astype(jnp.float32) + delta).astype(out_ref.dtype)


def finish(base, shrunk, ups, spot, live):
    rows, cols = base.shape
    rank = ups.shape[1]
    return pl.pallas_call(
        finish_body,
        grid_spec=pltpu.PrefetchScalarGridSpec(
            num_scalar_prefetch=2,
            grid=(rows // BLOCK,),
            in_specs=[
                pl.BlockSpec((BLOCK, cols), lambda b, spot, live: (b, 0)),
                pl.BlockSpec((1, BLOCK, 2 * rank), lambda b, spot, live: (spot[b] // 2, 0, 0)),
                pl.BlockSpec((1, rank, cols), lambda b, spot, live: (spot[b], 0, 0)),
            ],
            out_specs=pl.BlockSpec((BLOCK, cols), lambda b, spot, live: (b, 0)),
        ),
        out_shape=jax.ShapeDtypeStruct((rows, cols), base.dtype),
    )(spot, live, base, shrunk, ups)


def per_device(
    tokens,
    base_projection_weight,
    adapter_down_maps,
    adapter_up_maps,
    block_adapter_ids,
    adapter_storage_entry,
):
    req_count = lax.axis_size("req")
    tp_count = lax.axis_size("tp")
    my_req = lax.axis_index("req")
    row_count, feat_count = tokens.shape
    blk_count = row_count // BLOCK
    adapter_count = adapter_down_maps.shape[0]

    ids_all = block_adapter_ids.reshape(req_count, blk_count)
    stored = adapter_storage_entry[jnp.maximum(ids_all - 1, 0)]
    owner_all = jnp.where(ids_all > 0, stored // adapter_count, -1)
    local_all = stored % adapter_count
    block_pos = jnp.arange(blk_count, dtype=jnp.int32)
    before = block_pos[None, :] < block_pos[:, None]
    same_owner = owner_all[:, :, None] == owner_all[:, None, :]
    slot_all = jnp.sum(same_owner & before[None], axis=2)
    slot_ids = jnp.arange(CAP, dtype=jnp.int32)[:, None, None]
    incoming = (owner_all[None] == my_req) & (slot_all[None] == slot_ids)
    send_local = jnp.sum(jnp.where(incoming, local_all[None], 0), axis=2)
    ids_own = lax.dynamic_index_in_dim(ids_all, my_req, 0, keepdims=False)
    owner_own = lax.dynamic_index_in_dim(owner_all, my_req, 0, keepdims=False)
    slot_own = lax.dynamic_index_in_dim(slot_all, my_req, 0, keepdims=False)
    owner_ids = jnp.arange(req_count, dtype=jnp.int32)[None, :, None]
    outgoing = (owner_own[None, None] == owner_ids) & (slot_own[None, None] == slot_ids)
    blk_of = jnp.sum(jnp.where(outgoing, block_pos[None, None], 0), axis=2)
    live = (ids_own > 0).astype(jnp.int32)
    spot = jnp.where(ids_own > 0, slot_own * req_count + owner_own, 0)

    swap = functools.partial(lax.all_to_all, axis_name="req", split_axis=0, concat_axis=0, tiled=True)
    downs = [swap(adapter_down_maps[send_local[s]]) for s in range(CAP)]
    ups = [swap(adapter_up_maps[send_local[s]]) for s in range(CAP)]

    partial_value = jnp.dot(tokens, base_projection_weight, preferred_element_type=jnp.float32)
    partial_value, blk_of = lax.optimization_barrier((partial_value.astype(jnp.bfloat16), blk_of))
    base = lax.psum_scatter(
        partial_value, "tp", scatter_dimension=1, tiled=True
    )

    split = tp_count // 2
    groups = [list(range(split)), list(range(split, tp_count))]
    shrunk = []
    for s in range(CAP):
        part = shrink_pairs(tokens, downs[s], blk_of[s])
        part = part.reshape((tp_count, part.shape[1] // split) + part.shape[2:])
        mine = lax.psum_scatter(part, "tp", scatter_dimension=0, tiled=False)
        shrunk.append(lax.all_gather(mine, "tp", axis_index_groups=groups, axis=0, tiled=True))
    return finish(base, jnp.concatenate(shrunk), jnp.concatenate(ups), spot, live)


def solution(mesh):
    placed = (P("req", "tp"), P("tp", None), P("req", "tp", None), P("req", None, "tp"), P(), P())
    return jax.shard_map(
        per_device, mesh=mesh, in_specs=placed, out_specs=P("req", "tp"), check_vma=False
    )
```

time: 344 us -> 349 us (1.015)
  Pallas kernels: 0 us -> 24.8 us
  waiting for transfers between devices: 246 us -> 233 us
  matrix products: 36 us -> 23.6 us
  other arithmetic: 12.5 us -> 4.19 us
  starting transfers between devices: 12.9 us -> 19.2 us
  blocking collectives: 0 us -> 3.92 us
  local copies, waits for them, and re-layouts: 21.9 us -> 25.6 us
    all_to_all x2 -> x4, waiting for transfers between devices: 222 us -> 173 us  [the longest x2 147 us: per_device(): downs = [swap(adapter_down_maps[send_local[s]]) for s in range(CAP)]]
    reduce_scatter x1, waiting for transfers between devices: 16.4 us -> 59.3 us  [per_device(): lax.psum_scatter(partial_value, 'tp', scatter_dimension=1, tiled=True)]
    pallas_call x0 -> x3, Pallas kernels: none -> 24.8 us  [the longest x1 12.4 us: finish(): pl.pallas_call(finish_body, grid_spec=pltpu.PrefetchScalarGridSpec(num_sc...]
    dot_general x2 -> x0, matrix products: 12.5 us -> none  [the longest x1 9.37 us: per_device(): jnp.einsum('vhyf,vhfp->vhyp', landed_rows, adapter_down_maps[input_reside...]
    psum x1 -> x0, waiting for transfers between devices: 7.84 us -> none  [per_device(): down_projected = lax.psum(partial_shrink.astype(jnp.bfloat16), 'tp')]
    select_n x3 -> x2, other arithmetic: 7.23 us -> 0.54 us  [the longest x1 0.53 us: per_device(): spot = jnp.where(ids_own > 0, slot_own * req_count + owner_own, 0)]
    all_to_all x2 -> x4, starting transfers between devices: 12.8 us -> 19.1 us  [the longest x2 11.9 us: per_device(): downs = [swap(adapter_down_maps[send_local[s]]) for s in range(CAP)]]
    all_gather x0 -> x2, blocking collectives: none -> 3.92 us  [per_device(): lax.all_gather(mine, 'tp', axis_index_groups=groups, axis=0, tiled=True)]
  transfers between devices with their start and end apart: 4 -> 6, of which waited for: 4 -> 5; matrix products, arithmetic and copies ran while one was open for 11% -> 12% of each run, Pallas kernels for 0% -> 2%
where the time goes in v1:
time: 349 us; the launch traced here: 348 us
  waiting for transfers between devices  233 us (67%)
  local copies, waits for them, and re-layouts  25.6 us (7%)
  Pallas kernels  24.8 us (7%)
  matrix products  23.6 us (7%)
  starting transfers between devices  19.2 us (6%)
  between operations  13.5 us (4%)
  other arithmetic  4.19 us (1%)
  blocking collectives  3.92 us (1%)
    all_to_all x2, waiting for transfers between devices, per_device(): downs = [swap(adapter_down_maps[send_local[s]]) for s in range(CAP)]  147 us
    reduce_scatter x1, waiting for transfers between devices, per_device(): lax.psum_scatter(partial_value, 'tp', scatter_dimension=1, tiled=True)  59.3 us
    all_to_all x2, waiting for transfers between devices, per_device(): ups = [swap(adapter_up_maps[send_local[s]]) for s in range(CAP)]  26.8 us
    dot_general x1, matrix products, per_device(): jnp.dot(tokens, base_projection_weight, preferred_element_type=jnp.float32)  23.6 us
    gather x2, local copies, waits for them, and re-layouts, per_device(): downs = [swap(adapter_down_maps[send_local[s]]) for s in range(CAP)]  12.8 us
    pallas_call x1, Pallas kernels, finish(): pl.pallas_call(finish_body, grid_spec=pltpu.PrefetchScalarGridSpec(num_sc...  12.4 us
    pallas_call x2, Pallas kernels, shrink_pairs(): pl.pallas_call(shrink_body, grid_spec=pltpu.PrefetchScalarGridSpec(num_sc...  12.4 us
    all_to_all x2, starting transfers between devices, per_device(): downs = [swap(adapter_down_maps[send_local[s]]) for s in range(CAP)]  11.9 us
  transfers between devices with their start and end apart: 6, of which 5 were waited for; matrix products, arithmetic and copies ran while one was open for 12% of the time, Pallas kernels for 2%

profile of v1, /device:TPU:0, one launch (start us, length us, event | category | flops | bytes accessed | tf_op | source)
XLA Modules:
  0.0 348.2 jit_solution(6948553421575973293)
XLA Ops:
  8.0 1.6 gather_fusion
  10.2 6.4 %gather_fusion.2 = bf16[8,2048,128]{2,1,0:T(8,128)(2,1)} fusion(bf16[16,2048,128]{2,1,0:T(8,128)(2,1)} %param.8, s32[1024]{0:T(1024)S(1)} %pad_clamp_fusion), kind=kCustom, calls=%fused_computation.2 | custom fusion | bytes 8388640 | tf_op jit(solution)/shard_map/gather | solution.py:115
  16.6 7.3 %all-to-all-start.1 = ((bf16[8,2048,128]{2,1,0:T(8,128)(2,1)}), bf16[8,2048,128]{2,1,0:T(8,128)(2,1)}, u32[]{:S(2)}, u32[]{:S(2)}) async-start(bf16[8,2048,128]{2,1,0:T(8,128)(2,1)} %gather_fusion.2), calls=%async_computation.2 | async-start | bytes 8388608 | tf_op jit(solution)/shard_map/all_to_all | solution.py:115
  23.9 6.4 %gather_fusion.1 = bf16[8,2048,128]{2,1,0:T(8,128)(2,1)} fusion(bf16[16,2048,128]{2,1,0:T(8,128)(2,1)} %param.8, s32[1024]{0:T(1024)S(1)} %pad_clamp_fusion.1), kind=kCustom, calls=%fused_computation.1 | custom fusion | bytes 8388640 | tf_op jit(solution)/shard_map/gather | solution.py:115
  30.3 86.8 %all-to-all-done.1.down_a.down_b = bf16[8,2048,128]{2,1,0:T(8,128)(2,1)} async-done(((bf16[8,2048,128]{2,1,0:T(8,128)(2,1)}), bf16[8,2048,128]{2,1,0:T(8,128)(2,1)}, u32[]{:S(2)}, u32[]{:S(2)}) %all-to-all-start.1) | async-done | bytes 4194336 | tf_op jit(solution)/shard_map/all_to_all | solution.py:115
  117.2 4.6 %all-to-all-start = ((bf16[8,2048,128]{2,1,0:T(8,128)(2,1)}), bf16[8,2048,128]{2,1,0:T(8,128)(2,1)}, u32[]{:S(2)}, u32[]{:S(2)}) async-start(bf16[8,2048,128]{2,1,0:T(8,128)(2,1)} %gather_fusion.1), calls=%async_computation.1 | async-start | bytes 8388608 | tf_op jit(solution)/shard_map/all_to_all | solution.py:115
  122.5 23.6 %convolution_convert_fusion = bf16[2048,2048]{1,0:T(8,128)(2,1)} fusion(bf16[2048,2048]{1,0:T(8,128)(2,1)} %tok_b.3, bf16[2048,2048]{1,0:T(8,128)(2,1)} %param.7), kind=kOutput, calls=%fused_computation.5 | convolution fusion | flops 17184063488 | bytes 25165824 | tf_op jit(solution)/shard_map/dot_general | solution.py:118
  146.7 6.2 %shard_map.65 = bf16[2,4,128,128]{3,2,1,0:T(8,128)(2,1)} custom-call(s32[8]{0:T(128)} %get-tuple-element.19.blk_ref, bf16[2048,2048]{1,0:T(8,128)(2,1)} %tok_b.3, bf16[2048,2048]{1,0:T(8,128)(2,1)} %tok_b.3, bf16[8,2048,128]{2,1,0:T(8,128)(2,1)} %all-to-all-done.1.down_a.down_b, bf16[8,2048,128]{2,1,0:T(8,128)(2,1)} %all-to-all-done.1.down_a.down_b), custom_call_target="tpu_custom_call" | custom-call | flops 536870912 | bytes 8388608 | tf_op jit(solution)/shard_map/pallas_call | solution.py:26
  152.8 1.7 copy.12
  154.5 59.8 %all-to-all-done.down_a.down_b = bf16[8,2048,128]{2,1,0:T(8,128)(2,1)} async-done(((bf16[8,2048,128]{2,1,0:T(8,128)(2,1)}), bf16[8,2048,128]{2,1,0:T(8,128)(2,1)}, u32[]{:S(2)}, u32[]{:S(2)}) %all-to-all-start) | async-done | bytes 4194336 | tf_op jit(solution)/shard_map/all_to_all | solution.py:115
  214.3 6.2 %shard_map.64 = bf16[2,4,128,128]{3,2,1,0:T(8,128)(2,1)} custom-call(s32[8]{0:T(128)} %get-tuple-element.18.blk_ref, bf16[2048,2048]{1,0:T(8,128)(2,1)} %tok_b.3, bf16[2048,2048]{1,0:T(8,128)(2,1)} %tok_b.3, bf16[8,2048,128]{2,1,0:T(8,128)(2,1)} %all-to-all-done.down_a.down_b, bf16[8,2048,128]{2,1,0:T(8,128)(2,1)} %all-to-all-done.down_a.down_b), custom_call_target="tpu_custom_call" | custom-call | flops 536870912 | bytes 8388608 | tf_op jit(solution)/shard_map/pallas_call | solution.py:26
  220.5 1.7 copy.11
  222.9 1.4 gather_fusion.4
  224.3 3.6 %all-to-all-start.3 = ((bf16[8,64,512]{2,1,0:T(8,128)(2,1)}), bf16[8,64,512]{2,1,0:T(8,128)(2,1)S(1)}, u32[]{:S(2)}, u32[]{:S(2)}) async-start(bf16[8,64,512]{2,1,0:T(8,128)(2,1)} %gather_fusion.4), calls=%async_computation.4 | async-start | bytes 1048576 | tf_op jit(solution)/shard_map/all_to_all | solution.py:116
  227.9 1.4 gather_fusion.3
  229.3 13.3 %all-to-all-done.3 = bf16[8,64,512]{2,1,0:T(8,128)(2,1)S(1)} async-done(((bf16[8,64,512]{2,1,0:T(8,128)(2,1)}), bf16[8,64,512]{2,1,0:T(8,128)(2,1)S(1)}, u32[]{:S(2)}, u32[]{:S(2)}) %all-to-all-start.3) | async-done | bytes 524320 | tf_op jit(solution)/shard_map/all_to_all | solution.py:116
  242.6 3.6 %all-to-all-start.2 = ((bf16[8,64,512]{2,1,0:T(8,128)(2,1)}), bf16[8,64,512]{2,1,0:T(8,128)(2,1)S(1)}, u32[]{:S(2)}, u32[]{:S(2)}) async-start(bf16[8,64,512]{2,1,0:T(8,128)(2,1)} %gather_fusion.3), calls=%async_computation.3 | async-start | bytes 1048576 | tf_op jit(solution)/shard_map/all_to_all | solution.py:116
  247.4 13.5 %all-to-all-done.2 = bf16[8,64,512]{2,1,0:T(8,128)(2,1)S(1)} async-done(((bf16[8,64,512]{2,1,0:T(8,128)(2,1)}), bf16[8,64,512]{2,1,0:T(8,128)(2,1)S(1)}, u32[]{:S(2)}, u32[]{:S(2)}) %all-to-all-start.2) | async-done | bytes 524320 | tf_op jit(solution)/shard_map/all_to_all | solution.py:116
  262.0 1.5 constant_dynamic-slice_fusion
  263.5 2.0 all-gather.1
  265.5 1.5 constant_dynamic-slice_fusion.1
  267.0 2.0 all-gather
  269.7 59.3 %reduce-scatter.8.cloned.1.call-done.base_ref = bf16[2048,512]{1,0:T(8,128)(2,1)} async-done(((bf16[2048,2048]{1,0:T(8,128)(2,1)}), bf16[2048,512]{1,0:T(8,128)(2,1)}) %reduce-scatter.8.cloned.1.call-update) | async-done | bytes 2097168 | tf_op jit(solution)/shard_map/reduce_scatter | solution.py:120
  329.0 12.4 %shard_map.66 = bf16[2048,512]{1,0:T(8,128)(2,1)} custom-call(s32[16]{0:T(128)} %get-tuple-element.13.spot_ref, s32[16]{0:T(128)} %bitcast_convert_fusion.live_ref, bf16[2048,512]{1,0:T(8,128)(2,1)} %reduce-scatter.8.cloned.1.call-done.base_ref, bf16[8,128,128]{2,1,0:T(8,128)(2,1)} %pad_maximum_fusion.1.shrink_ref, bf16[16,64,512]{2,1,0:T(8,128)(2,1)} %pad_maximum_fusion.up_ref), custom_call_target="tpu_custom_call" | custom-call | tf_op jit(solution)/shard_map/pallas_call | solution.py:63
  (30 shorter events, 7.1 us)
Async XLA Ops:
  6.5 216.4 %copy-start = (bf16[16,64,512]{2,1,0:T(8,128)(2,1)S(1)}, bf16[16,64,512]{2,1,0:T(8,128)(2,1)}, u32[]{:S(2)}) copy-start(bf16[16,64,512]{2,1,0:T(8,128)(2,1)} %param.9) | copy-start | bytes 3145732
  16.6 100.6 %all-to-all-start.1 = ((bf16[8,2048,128]{2,1,0:T(8,128)(2,1)}), bf16[8,2048,128]{2,1,0:T(8,128)(2,1)}, u32[]{:S(2)}, u32[]{:S(2)}) async-start(bf16[8,2048,128]{2,1,0:T(8,128)(2,1)} %gather_fusion.2), calls=%async_computation.2 | async-start | bytes 8388608 | tf_op jit(solution)/shard_map/all_to_all | solution.py:115
  117.2 97.1 %all-to-all-start = ((bf16[8,2048,128]{2,1,0:T(8,128)(2,1)}), bf16[8,2048,128]{2,1,0:T(8,128)(2,1)}, u32[]{:S(2)}, u32[]{:S(2)}) async-start(bf16[8,2048,128]{2,1,0:T(8,128)(2,1)} %gather_fusion.1), calls=%async_computation.1 | async-start | bytes 8388608 | tf_op jit(solution)/shard_map/all_to_all | solution.py:115
  121.8 140.2 %all-reduce.5.cloned.1.call-start = ((), (), s32[]{:S(2)}) async-start(), calls=%async_computation.6 | async-start | bytes 1048576
  220.5 25.8 %copy-start.1 = (u32[32]{0:T(128)S(1)}, u32[32]{0:T(128)}, u32[]{:S(2)}) copy-start(u32[32]{0:T(128)} %constant.56) | copy-start | bytes 388
  222.2 106.8 %reduce-scatter.8.cloned.1.call-start = ((), (), s32[]{:S(2)}) async-start(), calls=%async_computation.5 | async-start | bytes 10485760 | tf_op jit(solution)/shard_map/reduce_scatter | solution.py:120
  224.3 18.3 %all-to-all-start.3 = ((bf16[8,64,512]{2,1,0:T(8,128)(2,1)}), bf16[8,64,512]{2,1,0:T(8,128)(2,1)S(1)}, u32[]{:S(2)}, u32[]{:S(2)}) async-start(bf16[8,64,512]{2,1,0:T(8,128)(2,1)} %gather_fusion.4), calls=%async_computation.4 | async-start | bytes 1048576 | tf_op jit(solution)/shard_map/all_to_all | solution.py:116
  242.6 18.3 %all-to-all-start.2 = ((bf16[8,64,512]{2,1,0:T(8,128)(2,1)}), bf16[8,64,512]{2,1,0:T(8,128)(2,1)S(1)}, u32[]{:S(2)}, u32[]{:S(2)}) async-start(bf16[8,64,512]{2,1,0:T(8,128)(2,1)} %gather_fusion.3), calls=%async_computation.3 | async-start | bytes 1048576 | tf_op jit(solution)/shard_map/all_to_all | solution.py:116
Sparse Core Ops, SparseCore 0:
  222.3 32.2 all-reduce.4
  257.1 71.7 reduce-scatter.7

commit v2 on v1

--- a/solution.py
+++ b/solution.py
@@ -10,6 +10,39 @@
 KEY_WIDTH = 1024
 BLOCK = 128
 CAP = 2
+LANES = 128
+MESH = pl.DeviceIdType.MESH
+
+
+def pack_body(idx_ref, down_ref, up_ref, out_ref):
+    feat = down_ref.shape[1]
+    rank = up_ref.shape[1]
+    out_ref[0, :feat] = down_ref[0]
+    for c in range(up_ref.shape[2] // LANES):
+        out_ref[0, feat + c * rank:feat + (c + 1) * rank] = up_ref[0, :, c * LANES:(c + 1) * LANES]
+
+
+def pack(downs, ups, idx):
+    count = idx.shape[0]
+    feat, width = downs.shape[1:]
+    rank, cols = ups.shape[1:]
+    rows = feat + rank * cols // LANES
+    return pl.pallas_call(
+        pack_body,
+        grid_spec=pltpu.PrefetchScalarGridSpec(
+            num_scalar_prefetch=1,
+            grid=(count,),
+            in_specs=[
+                pl.BlockSpec((1, feat, width), lambda p, idx: (idx[p], 0, 0)),
+                pl.BlockSpec((1, rank, cols), lambda p, idx: (idx[p], 0, 0)),
+            ],
+            out_specs=pl.BlockSpec((1, rows, width), lambda p, idx: (p, 0, 0)),
+        ),
+        out_shape=jax.ShapeDtypeStruct((count, rows, width), downs.dtype),
+        cost_estimate=pl.CostEstimate(
+            flops=0, bytes_accessed=4 * count * rows * width, transcendentals=0
+        ),
+    )(idx, downs, ups)
 
 
 def shrink_body(blk_ref, tok_a, tok_b, down_a, down_b, out_ref):
@@ -20,8 +53,9 @@
     out_ref[1, 0] = jnp.concatenate([one[:, rank:], two[:, rank:]], axis=1)
 
 
-def shrink_pairs(tokens, downs, blk_of):
-    items, feat, width = downs.shape
+def shrink_pairs(tokens, packed, blk_of):
+    items, _, width = packed.shape
+    feat = tokens.shape[1]
     pairs = items // 2
     return pl.pallas_call(
         shrink_body,
@@ -42,38 +76,98 @@
             bytes_accessed=2 * items * feat * (BLOCK + width),
             transcendentals=0,
         ),
-    )(blk_of, tokens, tokens, downs, downs)
-
-
-def finish_body(spot_ref, live_ref, base_ref, shrink_ref, up_ref, out_ref):
-    b = pl.program_id(0)
-    rank = up_ref.shape[1]
-    odd = spot_ref[b] % 2
-    both = shrink_ref[0]
-    mine = jnp.where(odd == 1, both[:, rank:], both[:, :rank])
-    delta = jnp.dot(mine, up_ref[0], preferred_element_type=jnp.float32)
-    delta = delta.astype(jnp.bfloat16).astype(jnp.float32)
-    delta = jnp.where(live_ref[b] > 0, delta, jnp.zeros_like(delta))
-    out_ref[...] = (base_ref[...].astype(jnp.float32) + delta).astype(out_ref.dtype)
-
-
-def finish(base, shrunk, ups, spot, live):
+    )(blk_of, tokens, tokens, packed, packed)
+
+
+def exchange_body(n, part_ref, out_ref, landed, send_sem, recv_sem):
+    me = lax.axis_index("tp")
+    barrier = pltpu.get_barrier_semaphore()
+    for d in range(1, n):
+        pl.semaphore_signal(
+            barrier, inc=1, device_id={"tp": lax.rem(me + d, n)}, device_id_type=MESH
+        )
+    pl.semaphore_wait(barrier, n - 1)
+    copies = []
+    for d in range(1, n):
+        to = lax.rem(me + d, n)
+        copy = pltpu.make_async_remote_copy(
+            src_ref=part_ref.at[to // (n // 2)],
+            dst_ref=landed.at[d - 1],
+            send_sem=send_sem.at[d - 1],
+            recv_sem=recv_sem.at[d - 1],
+            device_id={"tp": to},
+            device_id_type=MESH,
+        )
+        copy.start()
+        copies.append(copy)
+    for copy in copies:
+        copy.wait()
+    total = part_ref[me // (n // 2)].astype(jnp.float32)
+    for d in range(1, n):
+        total = total + landed[d - 1].astype(jnp.float32)
+    out_ref[...] = total.astype(out_ref.dtype)
+
+
+def exchange(part, n, collective_id):
+    shape = part.shape[1:]
+    return pl.pallas_call(
+        functools.partial(exchange_body, n),
+        out_shape=jax.ShapeDtypeStruct(shape, part.dtype),
+        in_specs=[pl.BlockSpec(memory_space=pltpu.VMEM)],
+        out_specs=pl.BlockSpec(memory_space=pltpu.VMEM),
+        scratch_shapes=[
+            pltpu.VMEM((n - 1,) + shape, part.dtype),
+            pltpu.SemaphoreType.DMA((n - 1,)),
+            pltpu.SemaphoreType.DMA((n - 1,)),
+        ],
+        compiler_params=pltpu.CompilerParams(collective_id=collective_id, has_side_effects=True),
+    )(part)
+
+
+def finish_body(req_count, per_step, spot_ref, live_ref, base_ref, s0, s1, u0, u1, out_ref):
+    rank = s0.shape[-1] // 2
+    for k in range(per_step):
+        b = pl.program_id(0) * per_step + k
+        spot = spot_ref[b]
+        second = spot // req_count == 1
+        owner = lax.rem(spot, req_count)
+        both = jnp.where(second, s1[owner // 2], s0[owner // 2])
+        mine = jnp.where(lax.rem(owner, 2) == 1, both[:, rank:], both[:, :rank])
+        up = jnp.where(second, u1[owner], u0[owner])
+        rows = slice(k * BLOCK, (k + 1) * BLOCK)
+        for c in range(out_ref.shape[1] // LANES):
+            delta = jnp.dot(
+                mine, up[c * rank:(c + 1) * rank], preferred_element_type=jnp.float32
+            )
+            delta = delta.astype(jnp.bfloat16).astype(jnp.float32)
+            delta = jnp.where(live_ref[b] > 0, delta, jnp.zeros_like(delta))
+            cols = slice(c * LANES, (c + 1) * LANES)
+            out_ref[rows, cols] = (base_ref[rows, cols].astype(jnp.float32) + delta).astype(
+                out_ref.dtype
+            )
+
+
+def finish(base, shrunk, packed, spot, live):
     rows, cols = base.shape
-    rank = ups.shape[1]
-    return pl.pallas_call(
-        finish_body,
+    items, total_rows, width = packed[0].shape
+    rank = width // 2
+    up_rows = rank * cols // LANES
+    per_step = 4
+    whole = pl.BlockSpec(shrunk[0].shape, lambda g, spot, live: (0, 0, 0))
+    ups = pl.BlockSpec(
+        (items, up_rows, width), lambda g, spot, live: (0, total_rows // up_rows - 1, 0)
+    )
+    mine = pl.BlockSpec((per_step * BLOCK, cols), lambda g, spot, live: (g, 0))
+    return pl.pallas_call(
+        functools.partial(finish_body, items, per_step),
         grid_spec=pltpu.PrefetchScalarGridSpec(
             num_scalar_prefetch=2,
-            grid=(rows // BLOCK,),
-            in_specs=[
-                pl.BlockSpec((BLOCK, cols), lambda b, spot, live: (b, 0)),
-                pl.BlockSpec((1, BLOCK, 2 * rank), lambda b, spot, live: (spot[b] // 2, 0, 0)),
-                pl.BlockSpec((1, rank, cols), lambda b, spot, live: (spot[b], 0, 0)),
-            ],
-            out_specs=pl.BlockSpec((BLOCK, cols), lambda b, spot, live: (b, 0)),
+            grid=(rows // (per_step * BLOCK),),
+            in_specs=[mine, whole, whole, ups, ups],
+            out_specs=mine,
         ),
         out_shape=jax.ShapeDtypeStruct((rows, cols), base.dtype),
-    )(spot, live, base, shrunk, ups)
+    )(spot, live, base, shrunk[0], shrunk[1], packed[0], packed[1])
 
 
 def per_device(
@@ -112,24 +206,22 @@
     spot = jnp.where(ids_own > 0, slot_own * req_count + owner_own, 0)
 
     swap = functools.partial(lax.all_to_all, axis_name="req", split_axis=0, concat_axis=0, tiled=True)
-    downs = [swap(adapter_down_maps[send_local[s]]) for s in range(CAP)]
-    ups = [swap(adapter_up_maps[send_local[s]]) for s in range(CAP)]
-
-    partial_value = jnp.dot(tokens, base_projection_weight, preferred_element_type=jnp.float32)
-    partial_value, blk_of = lax.optimization_barrier((partial_value.astype(jnp.bfloat16), blk_of))
-    base = lax.psum_scatter(
-        partial_value, "tp", scatter_dimension=1, tiled=True
-    )
-
-    split = tp_count // 2
-    groups = [list(range(split)), list(range(split, tp_count))]
-    shrunk = []
-    for s in range(CAP):
-        part = shrink_pairs(tokens, downs[s], blk_of[s])
-        part = part.reshape((tp_count, part.shape[1] // split) + part.shape[2:])
-        mine = lax.psum_scatter(part, "tp", scatter_dimension=0, tiled=False)
-        shrunk.append(lax.all_gather(mine, "tp", axis_index_groups=groups, axis=0, tiled=True))
-    return finish(base, jnp.concatenate(shrunk), jnp.concatenate(ups), spot, live)
+    sent = pack(adapter_down_maps, adapter_up_maps, send_local[0])
+    sent, later = lax.optimization_barrier((sent, send_local[1]))
+    first = swap(sent)
+    sent_later = pack(adapter_down_maps, adapter_up_maps, later)
+    sent_later, weight = lax.optimization_barrier((sent_later, base_projection_weight))
+    second = swap(sent_later)
+    partial_value = jnp.dot(tokens, weight, preferred_element_type=jnp.float32)
+    partial_value = partial_value.astype(jnp.bfloat16)
+    first, partial_value = lax.optimization_barrier((first, partial_value))
+    base = lax.psum_scatter(partial_value, "tp", scatter_dimension=1, tiled=True)
+
+    packed = [first, second]
+    shrunk = [
+        exchange(shrink_pairs(tokens, packed[s], blk_of[s]), tp_count, s) for s in range(CAP)
+    ]
+    return finish(base, shrunk, packed, spot, live)
 
 
 def solution(mesh):

time: 349 us -> 268 us (0.77)
  waiting for transfers between devices: 233 us -> 157 us
  Pallas kernels: 24.8 us -> 54.7 us
  local copies, waits for them, and re-layouts: 25.6 us -> 3.16 us
  starting transfers between devices: 19.2 us -> 12 us
  blocking collectives: 3.92 us -> 0 us
    reduce_scatter x1, waiting for transfers between devices: 59.3 us -> 0.02 us  [per_device(): lax.psum_scatter(partial_value, 'tp', scatter_dimension=1, tiled=True)]
    pallas_call x1 -> x5, Pallas kernels: 12.4 us -> 40.4 us  [the longest x2 19.7 us: exchange(): pl.pallas_call(functools.partial(exchange_body, n), out_shape=jax.ShapeDt...]
    all_to_all x4 -> x2, waiting for transfers between devices: 173 us -> 157 us  [the longest x1 83.9 us: per_device(): second = swap(sent_later)]
    gather x4 -> x0, local copies, waits for them, and re-layouts: 15.6 us -> none  [the longest x2 12.8 us: per_device(): downs = [swap(adapter_down_maps[send_local[s]]) for s in range(CAP)]]
    all_to_all x4 -> x2, starting transfers between devices: 19.1 us -> 11.9 us  [the longest x1 7.28 us: per_device(): first = swap(sent)]
    all_gather x2 -> x0, blocking collectives: 3.92 us -> none  [per_device(): lax.all_gather(mine, 'tp', axis_index_groups=groups, axis=0, tiled=True)]
    unnamed x7 -> x2, local copies, waits for them, and re-layouts: 3.64 us -> 0.01 us
  transfers between devices with their start and end apart: 6 -> 3, of which waited for: 5 -> 2; matrix products, arithmetic and copies ran while one was open for 12% -> 10% of each run, Pallas kernels for 2% -> 16%
where the time goes in v2:
time: 268 us; the launch traced here: 267 us
  waiting for transfers between devices  157 us (59%)
  Pallas kernels  54.7 us (20%)
  matrix products  23.6 us (9%)
  between operations  13.5 us (5%)
  starting transfers between devices  12 us (4%)
  local copies, waits for them, and re-layouts  3.16 us (1%)
    all_to_all x1, waiting for transfers between devices, per_device(): second = swap(sent_later)  83.9 us
    all_to_all x1, waiting for transfers between devices, per_device(): first = swap(sent)  73.4 us
    dot_general x1, matrix products, per_device(): partial_value = jnp.dot(tokens, weight, preferred_element_type=jnp.float32)  23.6 us
    pallas_call x2, Pallas kernels, exchange(): pl.pallas_call(functools.partial(exchange_body, n), out_shape=jax.ShapeDt...  19.7 us
    pallas_call x2, Pallas kernels, pack(): pl.pallas_call(pack_body, grid_spec=pltpu.PrefetchScalarGridSpec(num_scal...  14.9 us
    pallas_call x2, Pallas kernels, shrink_pairs(): pl.pallas_call(shrink_body, grid_spec=pltpu.PrefetchScalarGridSpec(num_sc...  14.3 us
    all_to_all x1, starting transfers between devices, per_device(): first = swap(sent)  7.28 us
    pallas_call x1, Pallas kernels, finish(): pl.pallas_call(functools.partial(finish_body, items, per_step), grid_spec...  5.89 us
  transfers between devices with their start and end apart: 3, of which 2 were waited for; matrix products, arithmetic and copies ran while one was open for 10% of the time, Pallas kernels for 16%

profile of v2, /device:TPU:0, one launch (start us, length us, event | category | flops | bytes accessed | tf_op | source)
XLA Modules:
  0.0 266.6 jit_solution(15136062276871452081)
XLA Ops:
  6.5 0.7 reshape.168
  7.3 0.7 add_maximum_fusion
  8.0 1.2 gather_fusion
  9.2 0.1 reshape.170
  9.3 0.3 convert_reduce_fusion
  9.6 0.2 select_reduce_fusion.1
  9.8 0.5 slice_bitcast_fusion.2
  10.3 7.4 %shard_map.64 = bf16[8,2304,128]{2,1,0:T(8,128)(2,1)} custom-call(s32[8]{0:T(128)} %get-tuple-element.25.idx_ref, bf16[16,2048,128]{2,1,0:T(8,128)(2,1)} %down_ref.3, bf16[16,64,512]{2,1,0:T(8,128)(2,1)} %up_ref.3), custom_call_target="tpu_custom_call" | custom-call | bytes 9437184 | tf_op jit(solution)/shard_map/pallas_call | solution.py:30
  17.7 7.3 %all-to-all-start = ((bf16[8,2304,128]{2,1,0:T(8,128)(2,1)}), bf16[8,2304,128]{2,1,0:T(8,128)(2,1)}, u32[]{:S(2)}, u32[]{:S(2)}) async-start(bf16[8,2304,128]{2,1,0:T(8,128)(2,1)} %shard_map.64), calls=%async_computation | async-start | bytes 9437184 | tf_op jit(solution)/shard_map/all_to_all | solution.py:211
  25.0 0.0 reduce-scatter.2.cloned.1.call-start
  25.1 7.5 %shard_map.65 = bf16[8,2304,128]{2,1,0:T(8,128)(2,1)} custom-call(s32[8]{0:T(128)} %get-tuple-element.12.idx_ref, bf16[16,2048,128]{2,1,0:T(8,128)(2,1)} %down_ref.3, bf16[16,64,512]{2,1,0:T(8,128)(2,1)} %up_ref.3), custom_call_target="tpu_custom_call" | custom-call | bytes 9437184 | tf_op jit(solution)/shard_map/pallas_call | solution.py:30
  32.5 23.6 %convert_bitcast_fusion = bf16[2048,2048]{1,0:T(8,128)(2,1)} fusion(bf16[2048,2048]{1,0:T(8,128)(2,1)} %tok_b.3, bf16[2048,2048]{1,0:T(8,128)(2,1)} %param.7), kind=kOutput, calls=%fused_computation.1 | convolution fusion | flops 17184063488 | bytes 25165824 | tf_op jit(solution)/shard_map/dot_general | solution.py:215
  56.1 73.4 %all-to-all-done.down_a.down_b.u0 = bf16[8,2304,128]{2,1,0:T(8,128)(2,1)} async-done(((bf16[8,2304,128]{2,1,0:T(8,128)(2,1)}), bf16[8,2304,128]{2,1,0:T(8,128)(2,1)}, u32[]{:S(2)}, u32[]{:S(2)}) %all-to-all-start) | async-done | bytes 4718624 | tf_op jit(solution)/shard_map/all_to_all | solution.py:211
  129.6 4.6 %all-to-all-start.1 = ((bf16[8,2304,128]{2,1,0:T(8,128)(2,1)}), bf16[8,2304,128]{2,1,0:T(8,128)(2,1)}, u32[]{:S(2)}, u32[]{:S(2)}) async-start(bf16[8,2304,128]{2,1,0:T(8,128)(2,1)} %shard_map.65), calls=%async_computation.2 | async-start | bytes 9437184 | tf_op jit(solution)/shard_map/all_to_all | solution.py:214
  134.2 0.6 bitcast_convert_fusion.live_ref
  134.8 0.5 bitcast_select_fusion
  135.3 0.1 select_reduce_fusion
  135.4 0.6 slice_bitcast_fusion
  136.0 7.7 %shard_map.66.part_ref = bf16[2,4,128,128]{3,2,1,0:T(8,128)(2,1)} custom-call(s32[8]{0:T(128)} %get-tuple-element.23.blk_ref, bf16[2048,2048]{1,0:T(8,128)(2,1)} %tok_b.3, bf16[2048,2048]{1,0:T(8,128)(2,1)} %tok_b.3, bf16[8,2304,128]{2,1,0:T(8,128)(2,1)} %all-to-all-done.down_a.down_b.u0, bf16[8,2304,128]{2,1,0:T(8,128)(2,1)} %all-to-all-done.down_a.down_b.u0), custom_call_target="tpu_custom_call" | custom-call | flops 536870912 | bytes 8388608 | tf_op jit(solution)/shard_map/pallas_call | solution.py:60
  143.7 10.3 %shard_map.67.s0 = bf16[4,128,128]{2,1,0:T(8,128)(2,1)} custom-call(bf16[2,4,128,128]{3,2,1,0:T(8,128)(2,1)} %shard_map.66.part_ref), custom_call_target="tpu_custom_call" | custom-call | tf_op jit(solution)/shard_map/pallas_call | solution.py:113
  154.0 83.9 %all-to-all-done.1.down_a.down_b.u1 = bf16[8,2304,128]{2,1,0:T(8,128)(2,1)} async-done(((bf16[8,2304,128]{2,1,0:T(8,128)(2,1)}), bf16[8,2304,128]{2,1,0:T(8,128)(2,1)}, u32[]{:S(2)}, u32[]{:S(2)}) %all-to-all-start.1) | async-done | bytes 4718624 | tf_op jit(solution)/shard_map/all_to_all | solution.py:214
  237.9 6.5 %shard_map.68.part_ref = bf16[2,4,128,128]{3,2,1,0:T(8,128)(2,1)} custom-call(s32[8]{0:T(128)} %get-tuple-element.22.blk_ref, bf16[2048,2048]{1,0:T(8,128)(2,1)} %tok_b.3, bf16[2048,2048]{1,0:T(8,128)(2,1)} %tok_b.3, bf16[8,2304,128]{2,1,0:T(8,128)(2,1)} %all-to-all-done.1.down_a.down_b.u1, bf16[8,2304,128]{2,1,0:T(8,128)(2,1)} %all-to-all-done.1.down_a.down_b.u1), custom_call_target="tpu_custom_call" | custom-call | flops 536870912 | bytes 8388608 | tf_op jit(solution)/shard_map/pallas_call | solution.py:60
  244.5 9.4 %shard_map.69.s1 = bf16[4,128,128]{2,1,0:T(8,128)(2,1)} custom-call(bf16[2,4,128,128]{3,2,1,0:T(8,128)(2,1)} %shard_map.68.part_ref), custom_call_target="tpu_custom_call" | custom-call | tf_op jit(solution)/shard_map/pallas_call | solution.py:113
  253.9 5.9 %shard_map.70 = bf16[2048,512]{1,0:T(8,128)(2,1)} custom-call(s32[16]{0:T(128)} %get-tuple-element.19.spot_ref, s32[16]{0:T(128)} %bitcast_convert_fusion.live_ref, bf16[2048,512]{1,0:T(8,128)(2,1)} %reduce-scatter.2.cloned.1.call-done.base_ref, bf16[4,128,128]{2,1,0:T(8,128)(2,1)} %shard_map.67.s0, bf16[4,128,128]{2,1,0:T(8,128)(2,1)} %shard_map.69.s1, ...), custom_call_target="tpu_custom_call" | custom-call | tf_op jit(solution)/shard_map/pallas_call | solution.py:161
  (10 shorter events, 0.1 us)
Async XLA Ops:
  6.5 1.4 copy-start
  17.7 111.8 %all-to-all-start = ((bf16[8,2304,128]{2,1,0:T(8,128)(2,1)}), bf16[8,2304,128]{2,1,0:T(8,128)(2,1)}, u32[]{:S(2)}, u32[]{:S(2)}) async-start(bf16[8,2304,128]{2,1,0:T(8,128)(2,1)} %shard_map.64), calls=%async_computation | async-start | bytes 9437184 | tf_op jit(solution)/shard_map/all_to_all | solution.py:211
  25.0 228.9 %reduce-scatter.2.cloned.1.call-start = ((), (), s32[]{:S(2)}) async-start(), calls=%async_computation.3 | async-start | bytes 10485760 | tf_op jit(solution)/shard_map/reduce_scatter | solution.py:218
  129.6 108.4 %all-to-all-start.1 = ((bf16[8,2304,128]{2,1,0:T(8,128)(2,1)}), bf16[8,2304,128]{2,1,0:T(8,128)(2,1)}, u32[]{:S(2)}, u32[]{:S(2)}) async-start(bf16[8,2304,128]{2,1,0:T(8,128)(2,1)} %shard_map.65), calls=%async_computation.2 | async-start | bytes 9437184 | tf_op jit(solution)/shard_map/all_to_all | solution.py:214
Sparse Core Ops, SparseCore 0:
  129.7 70.7 reduce-scatter.1

commit v3 on v2

--- a/solution.py
+++ b/solution.py
@@ -14,12 +14,27 @@
 MESH = pl.DeviceIdType.MESH
 
 
-def pack_body(idx_ref, down_ref, up_ref, out_ref):
+def pack_body(idx_ref, down_ref, up_ref, out_ref, sem):
     feat = down_ref.shape[1]
-    rank = up_ref.shape[1]
-    out_ref[0, :feat] = down_ref[0]
-    for c in range(up_ref.shape[2] // LANES):
-        out_ref[0, feat + c * rank:feat + (c + 1) * rank] = up_ref[0, :, c * LANES:(c + 1) * LANES]
+    rank, cols = up_ref.shape[1:]
+    copies = []
+    for p in range(out_ref.shape[0]):
+        entry = idx_ref[p]
+        copies.append(
+            pltpu.make_async_copy(down_ref.at[entry], out_ref.at[p, pl.ds(0, feat)], sem.at[p, 0])
+        )
+        for c in range(cols // LANES):
+            copies.append(
+                pltpu.make_async_copy(
+                    up_ref.at[entry, :, pl.ds(c * LANES, LANES)],
+                    out_ref.at[p, pl.ds(feat + c * rank, rank)],
+                    sem.at[p, 1 + c],
+                )
+            )
+    for copy in copies:
+        copy.start()
+    for copy in copies:
+        copy.wait()
 
 
 def pack(downs, ups, idx):
@@ -31,12 +46,10 @@
         pack_body,
         grid_spec=pltpu.PrefetchScalarGridSpec(
             num_scalar_prefetch=1,
-            grid=(count,),
-            in_specs=[
-                pl.BlockSpec((1, feat, width), lambda p, idx: (idx[p], 0, 0)),
-                pl.BlockSpec((1, rank, cols), lambda p, idx: (idx[p], 0, 0)),
-            ],
-            out_specs=pl.BlockSpec((1, rows, width), lambda p, idx: (p, 0, 0)),
+            grid=(1,),
+            in_specs=[pl.BlockSpec(memory_space=pl.ANY)] * 2,
+            out_specs=pl.BlockSpec(memory_space=pl.ANY),
+            scratch_shapes=[pltpu.SemaphoreType.DMA((count, 1 + cols // LANES))],
         ),
         out_shape=jax.ShapeDtypeStruct((count, rows, width), downs.dtype),
         cost_estimate=pl.CostEstimate(
@@ -45,83 +58,78 @@
     )(idx, downs, ups)
 
 
-def shrink_body(blk_ref, tok_a, tok_b, down_a, down_b, out_ref):
+def shrink_body(n, tok_ref, down_ref, out_ref, part, landed, send_sem, recv_sem):
+    p = pl.program_id(0)
+    pairs = part.shape[1]
     rank = out_ref.shape[-1] // 2
-    one = jnp.dot(tok_a[...], down_a[0], preferred_element_type=jnp.float32).astype(out_ref.dtype)
-    two = jnp.dot(tok_b[...], down_b[0], preferred_element_type=jnp.float32).astype(out_ref.dtype)
-    out_ref[0, 0] = jnp.concatenate([one[:, :rank], two[:, :rank]], axis=1)
-    out_ref[1, 0] = jnp.concatenate([one[:, rank:], two[:, rank:]], axis=1)
-
-
-def shrink_pairs(tokens, packed, blk_of):
+    me = lax.axis_index("tp")
+    barrier = pltpu.get_barrier_semaphore()
+
+    @pl.when(p == 0)
+    def _():
+        for d in range(1, n):
+            pl.semaphore_signal(
+                barrier, inc=1, device_id={"tp": lax.rem(me + d, n)}, device_id_type=MESH
+            )
+        pl.semaphore_wait(barrier, n - 1)
+
+    one = jnp.dot(tok_ref[0], down_ref[0], preferred_element_type=jnp.float32).astype(part.dtype)
+    two = jnp.dot(tok_ref[1], down_ref[1], preferred_element_type=jnp.float32).astype(part.dtype)
+    part[0, p] = jnp.concatenate([one[:, :rank], two[:, :rank]], axis=1)
+    part[1, p] = jnp.concatenate([one[:, rank:], two[:, rank:]], axis=1)
+
+    def copy_of(d, pair):
+        to = lax.rem(me + d, n)
+        return pltpu.make_async_remote_copy(
+            src_ref=part.at[to // (n // 2), pair],
+            dst_ref=landed.at[d - 1, pair],
+            send_sem=send_sem.at[d - 1, pair],
+            recv_sem=recv_sem.at[d - 1, pair],
+            device_id={"tp": to},
+            device_id_type=MESH,
+        )
+
+    for d in range(1, n):
+        copy_of(d, p).start()
+
+    @pl.when(p == pairs - 1)
+    def _():
+        for pair in range(pairs):
+            for d in range(1, n):
+                copy_of(d, pair).wait()
+            total = part[me // (n // 2), pair].astype(jnp.float32)
+            for d in range(1, n):
+                total = total + landed[d - 1, pair].astype(jnp.float32)
+            out_ref[pair] = total.astype(out_ref.dtype)
+
+
+def shrink(tok_blocks, packed, slot, n):
     items, _, width = packed.shape
-    feat = tokens.shape[1]
+    feat = tok_blocks.shape[2]
     pairs = items // 2
+    shape = (pairs, BLOCK, width)
     return pl.pallas_call(
-        shrink_body,
-        grid_spec=pltpu.PrefetchScalarGridSpec(
-            num_scalar_prefetch=1,
-            grid=(pairs,),
-            in_specs=[
-                pl.BlockSpec((BLOCK, feat), lambda p, blk: (blk[2 * p], 0)),
-                pl.BlockSpec((BLOCK, feat), lambda p, blk: (blk[2 * p + 1], 0)),
-                pl.BlockSpec((1, feat, width), lambda p, blk: (2 * p, 0, 0)),
-                pl.BlockSpec((1, feat, width), lambda p, blk: (2 * p + 1, 0, 0)),
-            ],
-            out_specs=pl.BlockSpec((2, 1, BLOCK, width), lambda p, blk: (0, p, 0, 0)),
-        ),
-        out_shape=jax.ShapeDtypeStruct((2, pairs, BLOCK, width), tokens.dtype),
+        functools.partial(shrink_body, n),
+        grid=(pairs,),
+        in_specs=[
+            pl.BlockSpec((2, BLOCK, feat), lambda p: (slot * pairs + p, 0, 0)),
+            pl.BlockSpec((2, feat, width), lambda p: (p, 0, 0)),
+        ],
+        out_specs=pl.BlockSpec(shape, lambda p: (0, 0, 0)),
+        out_shape=jax.ShapeDtypeStruct(shape, packed.dtype),
+        scratch_shapes=[
+            pltpu.VMEM((2,) + shape, packed.dtype),
+            pltpu.VMEM((n - 1,) + shape, packed.dtype),
+            pltpu.SemaphoreType.DMA((n - 1, pairs)),
+            pltpu.SemaphoreType.DMA((n - 1, pairs)),
+        ],
+        compiler_params=pltpu.CompilerParams(collective_id=slot, has_side_effects=True),
         cost_estimate=pl.CostEstimate(
             flops=2 * items * BLOCK * feat * width,
             bytes_accessed=2 * items * feat * (BLOCK + width),
             transcendentals=0,
         ),
-    )(blk_of, tokens, tokens, packed, packed)
-
-
-def exchange_body(n, part_ref, out_ref, landed, send_sem, recv_sem):
-    me = lax.axis_index("tp")
-    barrier = pltpu.get_barrier_semaphore()
-    for d in range(1, n):
-        pl.semaphore_signal(
-            barrier, inc=1, device_id={"tp": lax.rem(me + d, n)}, device_id_type=MESH
-        )
-    pl.semaphore_wait(barrier, n - 1)
-    copies = []
-    for d in range(1, n):
-        to = lax.rem(me + d, n)
-        copy = pltpu.make_async_remote_copy(
-            src_ref=part_ref.at[to // (n // 2)],
-            dst_ref=landed.at[d - 1],
-            send_sem=send_sem.at[d - 1],
-            recv_sem=recv_sem.at[d - 1],
-            device_id={"tp": to},
-            device_id_type=MESH,
-        )
-        copy.start()
-        copies.append(copy)
-    for copy in copies:
-        copy.wait()
-    total = part_ref[me // (n // 2)].astype(jnp.float32)
-    for d in range(1, n):
-        total = total + landed[d - 1].astype(jnp.float32)
-    out_ref[...] = total.astype(out_ref.dtype)
-
-
-def exchange(part, n, collective_id):
-    shape = part.shape[1:]
-    return pl.pallas_call(
-        functools.partial(exchange_body, n),
-        out_shape=jax.ShapeDtypeStruct(shape, part.dtype),
-        in_specs=[pl.BlockSpec(memory_space=pltpu.VMEM)],
-        out_specs=pl.BlockSpec(memory_space=pltpu.VMEM),
-        scratch_shapes=[
-            pltpu.VMEM((n - 1,) + shape, part.dtype),
-            pltpu.SemaphoreType.DMA((n - 1,)),
-            pltpu.SemaphoreType.DMA((n - 1,)),
-        ],
-        compiler_params=pltpu.CompilerParams(collective_id=collective_id, has_side_effects=True),
-    )(part)
+    )(tok_blocks, packed)
 
 
 def finish_body(req_count, per_step, spot_ref, live_ref, base_ref, s0, s1, u0, u1, out_ref):
@@ -210,17 +218,18 @@
     sent, later = lax.optimization_barrier((sent, send_local[1]))
     first = swap(sent)
     sent_later = pack(adapter_down_maps, adapter_up_maps, later)
-    sent_later, weight = lax.optimization_barrier((sent_later, base_projection_weight))
+    sent_later, weight, picked = lax.optimization_barrier(
+        (sent_later, base_projection_weight, blk_of.reshape(-1))
+    )
     second = swap(sent_later)
     partial_value = jnp.dot(tokens, weight, preferred_element_type=jnp.float32)
     partial_value = partial_value.astype(jnp.bfloat16)
-    first, partial_value = lax.optimization_barrier((first, partial_value))
+    tok_blocks = tokens.reshape(blk_count, BLOCK, feat_count)[picked]
+    first, partial_value, tok_blocks = lax.optimization_barrier((first, partial_value, tok_blocks))
     base = lax.psum_scatter(partial_value, "tp", scatter_dimension=1, tiled=True)
 
     packed = [first, second]
-    shrunk = [
-        exchange(shrink_pairs(tokens, packed[s], blk_of[s]), tp_count, s) for s in range(CAP)
-    ]
+    shrunk = [shrink(tok_blocks, packed[s], s, tp_count) for s in range(CAP)]
     return finish(base, shrunk, packed, spot, live)
 
 

time: 268 us -> 475 us (1.77)
  Pallas kernels: 54.7 us -> 319 us
  waiting for transfers between devices: 157 us -> 92.1 us
  local copies, waits for them, and re-layouts: 3.16 us -> 10.9 us
    pallas_call x2, Pallas kernels: 14.9 us -> 290 us  [pack(): pl.pallas_call(pack_body, grid_spec=pltpu.PrefetchScalarGridSpec(num_scal...]
    all_to_all x1, waiting for transfers between devices: 73.4 us -> 0.01 us  [per_device(): first = swap(sent)]
    pallas_call x4 -> x2, Pallas kernels: 33.9 us -> 22.5 us  [shrink(): pl.pallas_call(functools.partial(shrink_body, n), grid=(pairs,), in_specs...]
    all_to_all x1, waiting for transfers between devices: 83.9 us -> 92.1 us  [per_device(): second = swap(sent_later)]
    gather x0 -> x1, local copies, waits for them, and re-layouts: none -> 8.14 us  [per_device(): tok_blocks = tokens.reshape(blk_count, BLOCK, feat_count)[picked]]
  transfers between devices with their start and end apart: 3 -> 3, of which waited for: 2 -> 1; matrix products, arithmetic and copies ran while one was open for 10% -> 7% of each run, Pallas kernels for 16% -> 35%
where the time goes in v3:
time: 475 us; the launch traced here: 474 us
  Pallas kernels  319 us (67%)
  waiting for transfers between devices  92.1 us (19%)
  matrix products  23.5 us (5%)
  between operations  13.5 us (3%)
  starting transfers between devices  13.3 us (3%)
  local copies, waits for them, and re-layouts  10.9 us (2%)
    pallas_call x2, Pallas kernels, pack(): pl.pallas_call(pack_body, grid_spec=pltpu.PrefetchScalarGridSpec(num_scal...  290 us
    all_to_all x1, waiting for transfers between devices, per_device(): second = swap(sent_later)  92.1 us
    dot_general x1, matrix products, per_device(): partial_value = jnp.dot(tokens, weight, preferred_element_type=jnp.float32)  23.5 us
    pallas_call x2, Pallas kernels, shrink(): pl.pallas_call(functools.partial(shrink_body, n), grid=(pairs,), in_specs...  22.5 us
  transfers between devices with their start and end apart: 3, of which 1 were waited for; matrix products, arithmetic and copies ran while one was open for 7% of the time, Pallas kernels for 35%

profile of v3, /device:TPU:0, one launch (start us, length us, event | category | flops | bytes accessed | tf_op | source)
XLA Modules:
  0.0 474.3 jit_solution(1697749238319416581)
XLA Ops:
  6.5 0.7 add_maximum_fusion
  7.2 0.7 reshape.174
  8.0 1.2 gather_fusion
  9.2 0.1 reshape.178
  9.3 0.3 convert_reduce_fusion
  9.6 0.2 select_reduce_fusion.1
  9.7 0.6 slice_bitcast_fusion
  10.3 145.1 %shard_map.64 = bf16[8,2304,128]{2,1,0:T(8,128)(2,1)} custom-call(s32[8]{0:T(128)} %get-tuple-element.27.idx_ref, bf16[16,2048,128]{2,1,0:T(8,128)(2,1)} %down_ref.3, bf16[16,64,512]{2,1,0:T(8,128)(2,1)} %up_ref.3), custom_call_target="tpu_custom_call" | custom-call | bytes 9437184 | tf_op jit(solution)/shard_map/pallas_call | solution.py:45
  155.4 7.3 %all-to-all-start = ((bf16[8,2304,128]{2,1,0:T(8,128)(2,1)}), bf16[8,2304,128]{2,1,0:T(8,128)(2,1)}, u32[]{:S(2)}, u32[]{:S(2)}) async-start(bf16[8,2304,128]{2,1,0:T(8,128)(2,1)} %shard_map.64), calls=%async_computation | async-start | bytes 9437184 | tf_op jit(solution)/shard_map/all_to_all | solution.py:219
  162.7 0.0 reduce-scatter.2.cloned.1.call-start
  162.8 0.6 bitcast_select_fusion
  163.4 0.1 select_reduce_fusion
  163.5 0.1 reshape.175
  163.6 145.1 %shard_map.65 = bf16[8,2304,128]{2,1,0:T(8,128)(2,1)} custom-call(s32[8]{0:T(128)} %get-tuple-element.14.idx_ref, bf16[16,2048,128]{2,1,0:T(8,128)(2,1)} %down_ref.3, bf16[16,64,512]{2,1,0:T(8,128)(2,1)} %up_ref.3), custom_call_target="tpu_custom_call" | custom-call | bytes 9437184 | tf_op jit(solution)/shard_map/pallas_call | solution.py:45
  308.7 8.1 %gather_fusion.1 = bf16[16,128,2048]{2,1,0:T(8,128)(2,1)} fusion(bf16[16,128,2048]{2,1,0:T(8,128)(2,1)} %bitcast.18, s32[1024]{0:T(1024)S(1)} %pad_clamp_fusion), kind=kCustom, calls=%fused_computation.1 | custom fusion | bytes 16777280 | tf_op jit(solution)/shard_map/gather | solution.py:227
  316.8 23.5 %convert_bitcast_fusion = bf16[2048,2048]{1,0:T(8,128)(2,1)} fusion(bf16[2048,2048]{1,0:T(8,128)(2,1)} %param.6, bf16[2048,2048]{1,0:T(8,128)(2,1)} %param.7), kind=kOutput, calls=%fused_computation.2 | convolution fusion | flops 17184063488 | bytes 25165824 | tf_op jit(solution)/shard_map/dot_general | solution.py:225
  340.4 0.0 reduce-scatter.2.cloned.1.call-update
  340.4 6.0 %all-to-all-start.1 = ((bf16[8,2304,128]{2,1,0:T(8,128)(2,1)}), bf16[8,2304,128]{2,1,0:T(8,128)(2,1)}, u32[]{:S(2)}, u32[]{:S(2)}) async-start(bf16[8,2304,128]{2,1,0:T(8,128)(2,1)} %shard_map.65), calls=%async_computation.2 | async-start | bytes 9437184 | tf_op jit(solution)/shard_map/all_to_all | solution.py:224
  346.4 0.6 bitcast_convert_fusion.live_ref
  346.9 11.3 %shard_map.66.s0 = bf16[4,128,128]{2,1,0:T(8,128)(2,1)} custom-call(bf16[16,128,2048]{2,1,0:T(8,128)(2,1)} %gather_fusion.1, bf16[8,2304,128]{2,1,0:T(8,128)(2,1)} %all-to-all-done.down_ref.u0), custom_call_target="tpu_custom_call" | custom-call | flops 536870912 | bytes 8388608 | tf_op jit(solution)/shard_map/pallas_call | solution.py:111
  358.3 92.1 %all-to-all-done.1.down_ref.u1 = bf16[8,2304,128]{2,1,0:T(8,128)(2,1)} async-done(((bf16[8,2304,128]{2,1,0:T(8,128)(2,1)}), bf16[8,2304,128]{2,1,0:T(8,128)(2,1)}, u32[]{:S(2)}, u32[]{:S(2)}) %all-to-all-start.1) | async-done | bytes 4718624 | tf_op jit(solution)/shard_map/all_to_all | solution.py:224
  450.3 11.2 %shard_map.67.s1 = bf16[4,128,128]{2,1,0:T(8,128)(2,1)} custom-call(bf16[16,128,2048]{2,1,0:T(8,128)(2,1)} %gather_fusion.1, bf16[8,2304,128]{2,1,0:T(8,128)(2,1)} %all-to-all-done.1.down_ref.u1), custom_call_target="tpu_custom_call" | custom-call | flops 536870912 | bytes 8388608 | tf_op jit(solution)/shard_map/pallas_call | solution.py:111
  461.6 0.0 reduce-scatter.2.cloned.1.call-done.base_ref
  461.6 5.9 %shard_map.68 = bf16[2048,512]{1,0:T(8,128)(2,1)} custom-call(s32[16]{0:T(128)} %get-tuple-element.23.spot_ref, s32[16]{0:T(128)} %bitcast_convert_fusion.live_ref, bf16[2048,512]{1,0:T(8,128)(2,1)} %reduce-scatter.2.cloned.1.call-done.base_ref, bf16[4,128,128]{2,1,0:T(8,128)(2,1)} %shard_map.66.s0, bf16[4,128,128]{2,1,0:T(8,128)(2,1)} %shard_map.67.s1, ...), custom_call_target="tpu_custom_call" | custom-call | tf_op jit(solution)/shard_map/pallas_call | solution.py:169
  (11 shorter events, 0.1 us)
Async XLA Ops:
  6.5 1.4 copy-start
  155.4 185.0 %all-to-all-start = ((bf16[8,2304,128]{2,1,0:T(8,128)(2,1)}), bf16[8,2304,128]{2,1,0:T(8,128)(2,1)}, u32[]{:S(2)}, u32[]{:S(2)}) async-start(bf16[8,2304,128]{2,1,0:T(8,128)(2,1)} %shard_map.64), calls=%async_computation | async-start | bytes 9437184 | tf_op jit(solution)/shard_map/all_to_all | solution.py:219
  162.7 298.9 %reduce-scatter.2.cloned.1.call-start = ((), (), s32[]{:S(2)}) async-start(), calls=%async_computation.3 | async-start | bytes 10485760 | tf_op jit(solution)/shard_map/reduce_scatter | solution.py:229
  340.4 109.9 %all-to-all-start.1 = ((bf16[8,2304,128]{2,1,0:T(8,128)(2,1)}), bf16[8,2304,128]{2,1,0:T(8,128)(2,1)}, u32[]{:S(2)}, u32[]{:S(2)}) async-start(bf16[8,2304,128]{2,1,0:T(8,128)(2,1)} %shard_map.65), calls=%async_computation.2 | async-start | bytes 9437184 | tf_op jit(solution)/shard_map/all_to_all | solution.py:224
Sparse Core Ops, SparseCore 0:
  340.5 73.0 reduce-scatter.1
